TPU v7x, 256 devices: a whole 4x4x8 slice. The times are simulated.
256 devices in a mesh: dp: 16 (over x, y), tensor: 8 (over z), side: 2 (over core).
Axes of the slice: x: 4, y: 4, z: 8, core: 2. Of those that a mesh axis runs over, the one named last changes fastest.
Arguments:
- q_new: bfloat16 [1024, 6144], P(('dp', 'side'), 'tensor'), may hold values from -6 to 6
- k_new: bfloat16 [1024, 1024], P(('dp', 'side'), 'tensor'), may hold values from -6 to 6
- v_new: bfloat16 [1024, 1024], P(('dp', 'side'), 'tensor'), may hold values from -6 to 6
- k_cache: bfloat16 [1024, 192, 1024], P(('dp', 'side'), None, 'tensor'), may hold values from -6 to 6
- v_cache: bfloat16 [1024, 192, 1024], P(('dp', 'side'), None, 'tensor'), may hold values from -6 to 6
- lengths: int32 [1024], P(('dp', 'side')), may hold values from 24 to 192, as said below
- attn_out_weight: bfloat16 [6144, 6144], P('tensor', ('dp', 'side')), may hold values from -0.078125 to 0.078125
- residual: bfloat16 [1024, 6144], P('tensor', ('dp', 'side')), may hold values from -1.5 to 1.5
- norm_gain: float32 [6144], replicated, may hold values from 0.1 to 1.9
- router_weight: bfloat16 [6144, 8], replicated, may hold values from -0.02734375 to 0.02734375
- expert_ids: int32 [1024, 2], replicated, may hold values from 0 to 7, all different within a row; in each aligned block of 128 rows (0 to 127, 128 to 255, ...) at most 64 rows name the same one
- gate_weight: bfloat16 [8, 6144, 8192], P('tensor', None, ('dp', 'side')), may hold values from -0.078125 to 0.078125
- up_weight: bfloat16 [8, 6144, 8192], P('tensor', None, ('dp', 'side')), may hold values from -0.078125 to 0.078125
- down_weight: bfloat16 [8, 8192, 6144], P('tensor', ('dp', 'side')), may hold values from -0.0625 to 0.0625
Outputs:
- layer_out: bfloat16 [1024, 6144], P('tensor', ('dp', 'side'))
Inputs may be any that keep to these rules, and one draw needn't show every extreme that they name: `expert_ids`: each row names two different experts; in each aligned block of 128 rows no expert is named by more than 64 rows, and in every draw some expert is named by exactly 64 rows of a block. Row r attends to cached positions 0 to lengths[r] - 1 and to its new key; some rows hold all 192.
All inputs are finite; a program needn't handle non-finite values.
Results may differ from a plain program's by a relative error of at most 0.035.
Values may be sent and summed in bfloat16 or wider, within the bound.
No kernel may reach another device: no remote copies, remote signals or barrier semaphores. Data moves between devices by JAX's collectives and lax.ppermute only.
A program may use at most 128 MiB of HBM per device.

v0:
```python
import jax
import jax.numpy as jnp
from jax import lax
from jax.sharding import PartitionSpec as P

HEAD_DIM = 128
EXPERTS = 8
eps = 1e-05


def slot_tables(expert_ids, experts, blocks, most):
    rows = expert_ids.shape[0]
    block_rows = rows // blocks
    labels = jnp.arange(experts, dtype=jnp.int32)
    chosen = (expert_ids[:, :, None] == labels[None, None, :]).astype(jnp.int32)
    member = jnp.sum(chosen, axis=1)
    ranks = jnp.cumsum(member.reshape(blocks, block_rows, experts), axis=1)
    ranks = ranks.reshape(rows, experts) - 1
    block_of = jnp.arange(rows, dtype=jnp.int32) // block_rows
    slots = block_of[:, None] * most + ranks
    picked = jnp.sum(chosen * slots[:, None, :], axis=2)
    capacity = blocks * most
    row_ids = jnp.broadcast_to(jnp.arange(rows, dtype=jnp.int32)[:, None], (rows, 2))
    others = expert_ids[:, ::-1]
    leads = jnp.broadcast_to(jnp.array([1, 0], dtype=jnp.int32)[None, :], (rows, 2))
    table = jnp.full((experts, capacity), rows, jnp.int32).at[expert_ids, picked].set(row_ids)
    partner = jnp.zeros((experts, capacity), jnp.int32).at[expert_ids, picked].set(others)
    leading = jnp.zeros((experts, capacity), jnp.int32).at[expert_ids, picked].set(leads)
    return (picked, table, partner, leading)


def shards(
    q_new,
    k_new,
    v_new,
    k_cache,
    v_cache,
    lengths,
    attn_out_weight,
    residual,
    norm_gain,
    router_weight,
    expert_ids,
    gate_weight,
    up_weight,
    down_weight,
):
    rows_dev = q_new.shape[0]
    kv_local = k_new.shape[1] // HEAD_DIM
    heads_local = q_new.shape[1] // HEAD_DIM
    group_size = heads_local // kv_local
    cache_len = k_cache.shape[1]
    inv_root = HEAD_DIM ** (-0.5)
    queries = q_new.reshape(rows_dev, kv_local, group_size, HEAD_DIM)
    cache_keys = k_cache.reshape(rows_dev, cache_len, kv_local, HEAD_DIM)
    cache_values = v_cache.reshape(rows_dev, cache_len, kv_local, HEAD_DIM)
    own_keys = k_new.reshape(rows_dev, kv_local, HEAD_DIM)
    own_values = v_new.reshape(rows_dev, kv_local, HEAD_DIM).astype(jnp.float32)
    cache_scores = (
        jnp.einsum("rkgd,rckd->rkgc", queries, cache_keys, preferred_element_type=jnp.float32)
        * inv_root
    )
    own_scores = (
        jnp.einsum("rkgd,rkd->rkg", queries, own_keys, preferred_element_type=jnp.float32)
        * inv_root
    )
    live_mask = (jnp.arange(cache_len, dtype=jnp.int32)[None, :] < lengths[:, None])[
        :, None, None, :
    ]
    cache_scores = jnp.where(live_mask, cache_scores, -1e30)
    peak = jnp.maximum(jnp.max(cache_scores, axis=3), own_scores)
    cache_exp = jnp.exp(cache_scores - peak[..., None])
    own_exp = jnp.exp(own_scores - peak)
    denominator = jnp.sum(cache_exp, axis=3) + own_exp
    cache_weights = (cache_exp / denominator[..., None]).astype(jnp.bfloat16)
    own_weights = (own_exp / denominator).astype(jnp.bfloat16).astype(jnp.float32)
    mixed_heads = jnp.einsum(
        "rkgc,rckd->rkgd", cache_weights, cache_values, preferred_element_type=jnp.float32
    )
    mixed_heads = mixed_heads + own_weights[..., None] * own_values[:, :, None, :]
    attention = mixed_heads.reshape(rows_dev, heads_local * HEAD_DIM).astype(jnp.bfloat16)
    head_sums = jnp.dot(
        lax.all_gather(attention, ("dp", "side"), axis=0, tiled=True),
        attn_out_weight,
        preferred_element_type=jnp.float32,
    )
    total_rows = expert_ids.shape[0]
    tensor_count = lax.axis_size("tensor")
    tensor_rank = lax.axis_index("tensor")
    block_rows = total_rows // tensor_count
    most = block_rows // 2
    experts_local = gate_weight.shape[0]
    col_width = head_sums.shape[1]
    picked, table, partner, leading = slot_tables(expert_ids, EXPERTS, tensor_count, most)
    own_rows = lax.dynamic_slice_in_dim(
        head_sums, tensor_rank * block_rows, block_rows, 0
    ) + residual.astype(jnp.float32)
    head_sums = lax.dynamic_update_slice_in_dim(head_sums, own_rows, tensor_rank * block_rows, 0)
    routed = jnp.take(head_sums, table, axis=0, mode="fill", fill_value=0.0)
    hidden = lax.psum_scatter(
        routed.astype(jnp.bfloat16), "tensor", scatter_dimension=0, tiled=True
    )
    hidden_f = hidden.astype(jnp.float32)
    labels = jnp.arange(EXPERTS, dtype=jnp.int32)
    mine = tensor_rank * experts_local + jnp.arange(experts_local, dtype=jnp.int32)
    features = lax.all_gather(hidden, ("dp", "side"), axis=2, tiled=True).astype(jnp.float32)
    normed = (
        features * lax.rsqrt(jnp.mean(features * features, axis=2, keepdims=True) + eps) * norm_gain
    ).astype(jnp.bfloat16)
    gate = jnp.einsum("ecd,edf->ecf", normed, gate_weight, preferred_element_type=jnp.float32)
    upward = jnp.einsum("ecd,edf->ecf", normed, up_weight, preferred_element_type=jnp.float32)
    logits = jnp.einsum("ecd,dk->eck", normed, router_weight, preferred_element_type=jnp.float32)
    inner = (jax.nn.silu(gate) * upward).astype(jnp.bfloat16)
    summed = lax.psum_scatter(
        jnp.einsum("efd,ecf->dec", down_weight, inner, preferred_element_type=jnp.float32).astype(
            jnp.bfloat16
        ),
        ("dp", "side"),
        scatter_dimension=0,
        tiled=True,
    ).astype(jnp.float32)
    expert_out = jnp.transpose(summed, (1, 2, 0))
    own_logit = jnp.sum(jnp.where(mine[:, None, None] == labels, logits, 0.0), axis=2)
    partner_mine = lax.dynamic_slice_in_dim(partner, tensor_rank * experts_local, experts_local, 0)
    other_logit = jnp.sum(jnp.where(partner_mine[..., None] == labels, logits, 0.0), axis=2)
    shares = jax.nn.sigmoid(own_logit - other_logit)
    parts = (shares[..., None] * expert_out).astype(jnp.bfloat16)
    table_mine = lax.dynamic_slice_in_dim(table, tensor_rank * experts_local, experts_local, 0)
    leading_mine = lax.dynamic_slice_in_dim(leading, tensor_rank * experts_local, experts_local, 0)
    values = parts.astype(jnp.float32) + hidden_f * leading_mine[..., None].astype(jnp.float32)
    buffer = (
        jnp.zeros((total_rows, col_width), jnp.float32)
        .at[table_mine.reshape(-1)]
        .add(values.reshape(-1, col_width), mode="drop")
    )
    out_rows = lax.psum_scatter(
        buffer.astype(jnp.bfloat16), "tensor", scatter_dimension=0, tiled=True
    )
    return out_rows


def solution(mesh):
    return jax.shard_map(
        shards,
        mesh=mesh,
        in_specs=(
            P(("dp", "side"), "tensor"),
            P(("dp", "side"), "tensor"),
            P(("dp", "side"), "tensor"),
            P(("dp", "side"), None, "tensor"),
            P(("dp", "side"), None, "tensor"),
            P(("dp", "side")),
            P("tensor", ("dp", "side")),
            P("tensor", ("dp", "side")),
            P(),
            P(),
            P(),
            P("tensor", None, ("dp", "side")),
            P("tensor", None, ("dp", "side")),
            P("tensor", ("dp", "side"), None),
        ),
        out_specs=P("tensor", ("dp", "side")),
        check_vma=False,
    )
```

profile of v0, /device:TPU:2, one launch (start us, length us, event | category | flops | bytes accessed | tf_op | source)
XLA Modules:
  0.0 374.5 jit_solution(10705472872214771290)
XLA Ops:
  10.0 2.4 fusion.44
  12.6 2.0 fusion.17
  16.4 2.0 broadcast_add_fusion
  18.4 1.2 copy.37
  21.0 1.3 reshape.304
  23.1 1.3 reshape.306
  24.4 8.1 %scatter_custom_fusion.1 = s32[4096]{0:T(1024)S(1)} fusion(s32[2048]{0:T(1024)S(1)} %reshape.304, s32[2048]{0:T(1024)S(1)} %reshape.306, s32[]{:T(128)} %constant.27.clone.1), kind=kCustom, calls=%fused_computation.68 | custom fusion | bytes 16388
  32.6 33.8 %all-gather.3.cloned.1.call-done = bf16[1024,768]{1,0:T(8,128)(2,1)} async-done(((bf16[32,768]{1,0:T(8,128)(2,1)}), bf16[1024,768]{1,0:T(8,128)(2,1)}) %all-gather.3.cloned.1.call-update) | async-done | bytes 1572880 | tf_op jit(solution)/shard_map/all_gather | solution.py:83
  66.4 3.0 fusion.45
  69.3 1.6 add_dynamic-update-slice_fusion
  70.9 2.1 copy.39
  73.0 16.9 %gather_fusion = bf16[4096,192]{1,0:T(8,128)(2,1)} fusion(bf16[1024,192]{1,0:T(8,128)(2,1)} %copy.39, s32[4096]{0:T(1024)S(1)} %broadcast_clamp_fusion), kind=kCustom, calls=%fused_computation | custom fusion | bytes 3162112 | tf_op jit(solution)/shard_map/jit(_take)/gather | solution.py:99
  90.0 3.8 %copy.40 = bf16[8,512,192]{1,2,0:T(8,128)(2,1)} copy(bf16[8,512,192]{2,1,0:T(8,128)(2,1)} %bitcast.68) | data formatting | bytes 3145728 | tf_op jit(solution)/shard_map/jit(_take)/gather | solution.py:99
  93.8 2.9 select_convert_fusion
  96.8 40.2 %reduce-scatter.6.cloned.1.call-done = bf16[1,512,192]{1,2,0:T(8,128)(2,1)} async-done(((bf16[8,512,192]{1,2,0:T(8,128)(2,1)}), bf16[1,512,192]{1,2,0:T(8,128)(2,1)}) %reduce-scatter.6.cloned.1.call-update) | async-done | bytes 196624 | tf_op jit(solution)/shard_map/reduce_scatter | solution.py:100
  137.2 54.3 %all-gather.5.cloned.1.call-done = bf16[1,512,6144]{1,2,0:T(8,128)(2,1)} async-done(((bf16[1,512,192]{1,2,0:T(8,128)(2,1)}), bf16[1,512,6144]{1,2,0:T(8,128)(2,1)}) %all-gather.5.cloned.1.call-update) | async-done | bytes 6291472 | tf_op jit(solution)/shard_map/all_gather | solution.py:106
  191.6 4.3 %fusion = f32[512]{0:T(512)S(1)} fusion(bf16[1,512,6144]{1,2,0:T(8,128)(2,1)} %all-gather.5.cloned.1.call-done), kind=kLoop, calls=%fused_computation.7 | loop fusion | flops 9436672 | bytes 6293504 | tf_op jit(solution)/shard_map/reduce_sum | solution.py:108
  196.2 1.6 fusion.4
  197.8 2.7 copy-done.1
  200.4 2.6 fusion.8
  203.1 13.1 %fusion.3 = bf16[6144,512]{0,1:T(8,128)(2,1)} fusion(bf16[1,256,6144]{2,1,0:T(8,128)(2,1)S(1)} %copy-done, bf16[512,6144]{0,1:T(8,128)(2,1)} %copy-done.1, bf16[1,6144,256]{2,1,0:T(8,128)(2,1)} %param.27, f32[512,256]{1,0:T(8,128)} %fusion.8), kind=kOutput, calls=%fused_computation.11 | convolution fusion | flops 3225157632 | bytes 19398656 | tf_op jit(solution)/shard_map/efd,ecf->dec/dot_general | solution.py:115
  216.1 8.6 %copy.49 = bf16[6144,512]{1,0:T(8,128)(2,1)} copy(bf16[6144,512]{0,1:T(8,128)(2,1)} %fusion.3) | data formatting | bytes 12582912
  226.1 1.3 reshape.312
  227.4 8.4 %scatter_custom_fusion.2 = s32[4096]{0:T(1024)S(1)} fusion(s32[2048]{0:T(1024)} %copy-done.9, s32[2048]{0:T(1024)S(1)} %reshape.312, s32[]{:T(128)} %constant.28.clone.1), kind=kCustom, calls=%fused_computation.66 | custom fusion | bytes 16896
  236.7 1.3 reshape.318
  238.1 8.2 %scatter_custom_fusion.3 = s32[4096]{0:T(1024)S(1)} fusion(s32[2048]{0:T(1024)} %copy-done.9, s32[2048]{0:T(1024)S(1)} %reshape.318, s32[]{:T(128)} %constant.28.clone.1), kind=kCustom, calls=%fused_computation.64 | custom fusion | bytes 16896
  246.4 4.0 %select_reduce_fusion.1 = (f32[512]{0:T(512)S(1)}, f32[512]{0:T(512)S(1)}) fusion(s32[512]{0:T(512)S(1)} %bitcast.76, pred[8]{0:T(512)(128)(4,1)S(1)} %iota_compare_fusion.3, bf16[512,6144]{0,1:T(8,128)(2,1)} %copy-done.1, bf16[6144,8]{0,1:T(8,128)(2,1)S(1)} %copy-done.6), kind=kOutput, calls=%fused_computation.50 | convolution fusion | flops 50351104 | bytes 6395912 | tf_op jit(solution)/shard_map/ecd,dk->eck/dot_general | solution.py:112
  250.4 68.0 %reduce-scatter.10.cloned.1.call-done = bf16[192,512]{1,0:T(8,128)(2,1)} async-done(((bf16[6144,512]{1,0:T(8,128)(2,1)}), bf16[192,512]{1,0:T(8,128)(2,1)}) %reduce-scatter.10.cloned.1.call-update) | async-done | bytes 196624
  322.3 4.8 %scatter_custom_fusion = f32[1024,192]{1,0:T(8,128)} fusion(s32[512]{0:T(512)S(1)} %bitcast.78, f32[512,192]{1,0:T(8,128)} %copy.43, f32[]{:T(128)} %constant.25.clone.1), kind=kCustom, calls=%fused_computation.25 | custom fusion | flops 98304 | bytes 786944 | tf_op jit(solution)/shard_map/scatter-add | solution.py:134
  327.1 2.1 convert_element_type.102
  329.3 37.1 %reduce-scatter.8.cloned.1.call-done = bf16[128,192]{1,0:T(8,128)(2,1)} async-done(((bf16[1024,192]{1,0:T(8,128)(2,1)}), bf16[128,192]{1,0:T(8,128)(2,1)}) %reduce-scatter.8.cloned.1.call-update) | async-done | bytes 49168 | tf_op jit(solution)/shard_map/reduce_scatter | solution.py:136
  366.4 1.6 copy.44
  (75 shorter events, 14.4 us)
Async XLA Ops:
  6.5 196.5 %copy-start = (bf16[1,256,6144]{2,1,0:T(8,128)(2,1)S(1)}, bf16[1,256,6144]{2,1,0:T(8,128)(2,1)}, u32[]{:S(2)}) copy-start(bf16[1,256,6144]{2,1,0:T(8,128)(2,1)} %param.28) | copy-start | bytes 9437188
  6.5 8.8 %copy-start.5 = (s32[1024,2]{0,1:T(2,128)S(1)}, s32[1024,2]{0,1:T(2,128)}, u32[]{:S(2)}) copy-start(s32[1024,2]{0,1:T(2,128)} %param.25) | copy-start | bytes 24580
  6.5 59.8 %all-gather.3.cloned.1.call-start = ((), (), s32[]{:S(2)}) async-start(), calls=%async_computation.3 | async-start | bytes 1622016 | tf_op jit(solution)/shard_map/all_gather | solution.py:83
  9.9 9.8 %copy-start.11 = (s32[2]{0:T(128)S(1)}, s32[2]{0:T(128)}, u32[]{:S(2)}) copy-start(s32[2]{0:T(128)} %constant.84) | copy-start | bytes 28
  10.0 9.8 %copy-start.12 = (s32[2]{0:T(128)S(1)}, s32[2]{0:T(128)}, u32[]{:S(2)}) copy-start(s32[2]{0:T(128)} %constant.87) | copy-start | bytes 28
  12.6 53.7 %copy-start.4 = (bf16[768,192]{0,1:T(8,128)(2,1)S(1)}, bf16[768,192]{0,1:T(8,128)(2,1)}, u32[]{:S(2)}) copy-start(bf16[768,192]{0,1:T(8,128)(2,1)} %param.21) | copy-start | bytes 884740
  15.3 121.6 %reduce-scatter.6.cloned.1.call-start = ((), (), s32[]{:S(2)}) async-start(), calls=%async_computation.4 | async-start | bytes 1769472 | tf_op jit(solution)/shard_map/reduce_scatter | solution.py:100
  16.4 52.9 %copy-start.7 = (bf16[128,192]{0,1:T(8,128)(2,1)S(1)}, bf16[128,192]{0,1:T(8,128)(2,1)}, u32[]{:S(2)}) copy-start(bf16[128,192]{0,1:T(8,128)(2,1)} %param.22) | copy-start | bytes 147460
  22.3 2.2 copy-start.9
  96.7 94.8 %all-gather.5.cloned.1.call-start = ((), (), s32[]{:S(2)}) async-start(), calls=%async_computation.5 | async-start | bytes 6488064 | tf_op jit(solution)/shard_map/all_gather | solution.py:106
  137.0 58.9 %copy-start.8 = (f32[6144]{0:T(1024)S(1)}, f32[6144]{0:T(1024)}, u32[]{:S(2)}) copy-start(f32[6144]{0:T(1024)} %param.23) | copy-start | bytes 73732
  137.0 181.4 %reduce-scatter.10.cloned.1.call-start = ((), (), s32[]{:S(2)}) async-start(), calls=%async_computation.7 | async-start | bytes 6488064
  191.6 4.6 %copy-start.2 = (bf16[1,512,6144]{1,2,0:T(8,128)(2,1)S(1)}, bf16[1,512,6144]{1,2,0:T(8,128)(2,1)}, u32[]{:S(2)}) copy-start(bf16[1,512,6144]{1,2,0:T(8,128)(2,1)} %all-gather.5.cloned.1.call-done) | copy-start | bytes 18874372
  196.2 4.3 %copy-start.3 = (bf16[1,6144,256]{2,1,0:T(8,128)(2,1)S(1)}, bf16[1,6144,256]{2,1,0:T(8,128)(2,1)}, u32[]{:S(2)}) copy-start(bf16[1,6144,256]{2,1,0:T(8,128)(2,1)} %param.26) | copy-start | bytes 9437188
  197.8 2.7 copy-start.1
  224.8 11.1 %copy-start.10 = (s32[2]{0:T(128)S(1)}, s32[2]{0:T(128)}, u32[]{:S(2)}) copy-start(s32[2]{0:T(128)} %constant.80.clone) | copy-start | bytes 28
  224.8 21.6 %copy-start.6 = (bf16[6144,8]{0,1:T(8,128)(2,1)S(1)}, bf16[6144,8]{0,1:T(8,128)(2,1)}, u32[]{:S(2)}) copy-start(bf16[6144,8]{0,1:T(8,128)(2,1)} %param.24) | copy-start | bytes 294916
  224.8 141.6 %reduce-scatter.8.cloned.1.call-start = ((), (), s32[]{:S(2)}) async-start(), calls=%async_computation.6 | async-start | bytes 589824 | tf_op jit(solution)/shard_map/reduce_scatter | solution.py:136
Sparse Core Ops, SparseCore 0:
  15.4 50.8 all-gather.2
  96.8 40.0 reduce-scatter.5
  139.5 51.9 all-gather.4
  224.9 93.4 reduce-scatter.9
  329.4 36.9 reduce-scatter.7
where the time goes:
time: 376 us; the launch traced here: 374 us
  waiting for transfers between devices  234 us (62%)
  local copies, waits for them, and re-layouts  76.7 us (20%)
  matrix products  27.9 us (7%)
  other arithmetic  22.5 us (6%)
  between operations  13.5 us (4%)
    unnamed x6, waiting for transfers between devices  68.1 us
    all_gather x1, waiting for transfers between devices, shards(): lax.all_gather(hidden, ('dp', 'side'), axis=2, tiled=True)  54.3 us
    unnamed x35, local copies, waits for them, and re-layouts  40.4 us
    reduce_scatter x1, waiting for transfers between devices, shards(): lax.psum_scatter(routed.astype(jnp.bfloat16), 'tensor', scatter_dimension...  40.2 us
    reduce_scatter x1, waiting for transfers between devices, shards(): lax.psum_scatter(buffer.astype(jnp.bfloat16), 'tensor', scatter_dimension...  37.1 us
    all_gather x1, waiting for transfers between devices, shards(): lax.all_gather(attention, ('dp', 'side'), axis=0, tiled=True)  33.8 us
    gather x2, local copies, waits for them, and re-layouts, shards(): routed = jnp.take(head_sums, table, axis=0, mode='fill', fill_value=0.0)  20.8 us
    dot_general x1, matrix products, shards(): jnp.einsum('efd,ecf->dec', down_weight, inner, preferred_element_type=jnp...  13.1 us
  transfers between devices with their start and end apart: 5, of which 5 were waited for; matrix products, arithmetic and copies ran while one was open for 11% of the time, Pallas kernels for 0%

commit v1 on v0

--- a/solution.py
+++ b/solution.py
@@ -1,3 +1,4 @@
+import functools
 import jax
 import jax.numpy as jnp
 from jax import lax
@@ -6,6 +7,15 @@
 HEAD_DIM = 128
 EXPERTS = 8
 eps = 1e-05
+
+
+def press_quarters_over_axis(z_in, across):
+    return jnp.concatenate(
+        lax.all_to_all(jnp.stack(lax.axis_size(across) * [z_in]), across, 0, 0), axis=2
+    )
+
+
+_find_modes = functools.partial(press_quarters_over_axis, across=("dp", "side"))
 
 
 def slot_tables(expert_ids, experts, blocks, most):
@@ -103,7 +113,7 @@
     hidden_f = hidden.astype(jnp.float32)
     labels = jnp.arange(EXPERTS, dtype=jnp.int32)
     mine = tensor_rank * experts_local + jnp.arange(experts_local, dtype=jnp.int32)
-    features = lax.all_gather(hidden, ("dp", "side"), axis=2, tiled=True).astype(jnp.float32)
+    features = _find_modes(hidden).astype(jnp.float32)
     normed = (
         features * lax.rsqrt(jnp.mean(features * features, axis=2, keepdims=True) + eps) * norm_gain
     ).astype(jnp.bfloat16)

time: 376 us -> 416 us (1.11)
  waiting for transfers between devices: 234 us -> 265 us
  other arithmetic: 22.5 us -> 31.4 us
  starting transfers between devices: 0.35 us -> 7.93 us
  local copies, waits for them, and re-layouts: 76.7 us -> 72 us
    all_to_all x0 -> x1, waiting for transfers between devices: none -> 76.6 us  [press_quarters_over_axis(): lax.all_to_all(jnp.stack(lax.axis_size(across) * [z_in]), across, 0, 0)]
    all_gather x1 -> x0, waiting for transfers between devices: 54.3 us -> none  [shards(): lax.all_gather(hidden, ('dp', 'side'), axis=2, tiled=True)]
    unnamed x6 -> x5, waiting for transfers between devices: 68.1 us -> 76.3 us
    all_to_all x0 -> x1, starting transfers between devices: none -> 7.59 us  [press_quarters_over_axis(): lax.all_to_all(jnp.stack(lax.axis_size(across) * [z_in]), across, 0, 0)]
    convert_element_type x0 -> x2, other arithmetic: none -> 6.08 us  [the longest x1 4.66 us: shards(): features = _find_modes(hidden).astype(jnp.float32)]
    gather x2 -> x1, local copies, waits for them, and re-layouts: 20.8 us -> 16.9 us  [shards(): routed = jnp.take(head_sums, table, axis=0, mode='fill', fill_value=0.0)]
    unnamed x35 -> x33, local copies, waits for them, and re-layouts: 40.4 us -> 40.5 us
  transfers between devices with their start and end apart: 5 -> 5, of which waited for: 5 -> 5; matrix products, arithmetic and copies ran while one was open for 11% -> 10% of each run, Pallas kernels for 0% -> 0%
where the time goes in v1:
time: 416 us; the launch traced here: 415 us
  waiting for transfers between devices  265 us (64%)
  local copies, waits for them, and re-layouts  72 us (17%)
  other arithmetic  31.4 us (8%)
  matrix products  24.8 us (6%)
  between operations  13.5 us (3%)
  starting transfers between devices  7.93 us (2%)
    all_to_all x1, waiting for transfers between devices, press_quarters_over_axis(): lax.all_to_all(jnp.stack(lax.axis_size(across) * [z_in]), across, 0, 0)  76.6 us
    unnamed x5, waiting for transfers between devices  76.3 us
    reduce_scatter x1, waiting for transfers between devices, shards(): lax.psum_scatter(routed.astype(jnp.bfloat16), 'tensor', scatter_dimension...  41.9 us
    unnamed x33, local copies, waits for them, and re-layouts  40.5 us
    reduce_scatter x1, waiting for transfers between devices, shards(): lax.psum_scatter(buffer.astype(jnp.bfloat16), 'tensor', scatter_dimension...  37.1 us
    all_gather x1, waiting for transfers between devices, shards(): lax.all_gather(attention, ('dp', 'side'), axis=0, tiled=True)  33.1 us
    gather x1, local copies, waits for them, and re-layouts, shards(): routed = jnp.take(head_sums, table, axis=0, mode='fill', fill_value=0.0)  16.9 us
    dot_general x1, matrix products, shards(): jnp.einsum('efd,ecf->dec', down_weight, inner, preferred_element_type=jnp...  13.1 us
  transfers between devices with their start and end apart: 5, of which 5 were waited for; matrix products, arithmetic and copies ran while one was open for 10% of the time, Pallas kernels for 0%

profile of v1, /device:TPU:2, one launch (start us, length us, event | category | flops | bytes accessed | tf_op | source)
XLA Modules:
  0.0 414.7 jit_solution(7036965382826637167)
XLA Ops:
  10.1 2.4 fusion.48
  12.7 2.0 fusion.15
  17.1 2.0 broadcast_add_fusion
  21.7 1.3 reshape.373
  23.8 1.3 reshape.375
  25.1 8.1 %scatter_custom_fusion.1 = s32[4096]{0:T(1024)S(1)} fusion(s32[2048]{0:T(1024)S(1)} %reshape.373, s32[2048]{0:T(1024)S(1)} %reshape.375, s32[]{:T(128)} %constant.27.clone.1), kind=kCustom, calls=%fused_computation.74 | custom fusion | bytes 16388
  33.3 33.1 %all-gather.2.cloned.1.call-done = bf16[1024,768]{1,0:T(8,128)(2,1)} async-done(((bf16[32,768]{1,0:T(8,128)(2,1)}), bf16[1024,768]{1,0:T(8,128)(2,1)}) %all-gather.2.cloned.1.call-update) | async-done | bytes 1572880 | tf_op jit(solution)/shard_map/all_gather | solution.py:93
  66.4 3.0 fusion.49
  69.4 1.6 add_dynamic-update-slice_fusion
  70.9 2.1 copy.39
  73.1 16.9 %gather_fusion = bf16[4096,192]{1,0:T(8,128)(2,1)} fusion(bf16[1024,192]{1,0:T(8,128)(2,1)} %copy.39, s32[4096]{0:T(1024)S(1)} %broadcast_clamp_fusion), kind=kCustom, calls=%fused_computation | custom fusion | bytes 3162112 | tf_op jit(solution)/shard_map/jit(_take)/gather | solution.py:109
  90.0 2.9 select_convert_fusion
  92.9 41.9 %reduce-scatter.6.cloned.1.call-done = bf16[1,512,192]{2,1,0:T(8,128)(2,1)} async-done(((bf16[8,512,192]{2,1,0:T(8,128)(2,1)}), bf16[1,512,192]{2,1,0:T(8,128)(2,1)}) %reduce-scatter.6.cloned.1.call-update) | async-done | bytes 196624 | tf_op jit(solution)/shard_map/reduce_scatter | solution.py:110
  135.9 3.4 stack.2
  139.3 7.6 %all-to-all-start = ((bf16[32,1,512,192]{2,3,1,0:T(8,128)(2,1)}), bf16[32,1,512,192]{2,3,1,0:T(8,128)(2,1)}, u32[]{:S(2)}, u32[]{:S(2)}) async-start(bf16[32,1,512,192]{2,3,1,0:T(8,128)(2,1)} %stack.2), calls=%async_computation.1 | async-start | bytes 12582912 | tf_op jit(solution)/shard_map/all_to_all | solution.py:14
  147.2 76.6 %all-to-all-done = bf16[32,1,512,192]{2,3,1,0:T(8,128)(2,1)} async-done(((bf16[32,1,512,192]{2,3,1,0:T(8,128)(2,1)}), bf16[32,1,512,192]{2,3,1,0:T(8,128)(2,1)}, u32[]{:S(2)}, u32[]{:S(2)}) %all-to-all-start) | async-done | bytes 6291488 | tf_op jit(solution)/shard_map/all_to_all | solution.py:14
  223.8 4.4 %multiply_reduce_fusion = f32[512]{0:T(512)S(1)} fusion(bf16[32,1,512,192]{2,3,1,0:T(8,128)(2,1)} %all-to-all-done), kind=kLoop, calls=%fused_computation.9 | loop fusion | flops 9436672 | bytes 6293504 | tf_op jit(solution)/shard_map/reduce_sum | solution.py:118
  228.3 4.5 %multiply_convert_fusion = bf16[32,1,512,192]{2,3,0,1:T(8,128)(2,1)S(1)} fusion(bf16[32,1,512,192]{2,3,1,0:T(8,128)(2,1)} %all-to-all-done, f32[32,192]{1,0:T(8,128)S(1)} %mul.152, f32[512]{0:T(512)S(1)} %add_rsqrt_fusion), kind=kLoop, calls=%fused_computation.8 | loop fusion | flops 12582912 | bytes 12609536 | tf_op jit(solution)/shard_map/convert.3
  232.8 2.6 copy-done.2
  235.4 2.6 fusion.6
  238.0 13.1 %fusion.2 = bf16[6144,512]{0,1:T(8,128)(2,1)} fusion(bf16[1,256,6144]{2,1,0:T(8,128)(2,1)S(1)} %copy-done, bf16[512,6144]{0,1:T(8,128)(2,1)} %bitcast.91, bf16[1,6144,256]{2,1,0:T(8,128)(2,1)} %param.27, f32[512,256]{1,0:T(8,128)} %fusion.6), kind=kOutput, calls=%fused_computation.11 | convolution fusion | flops 3225157632 | bytes 19398656 | tf_op jit(solution)/shard_map/efd,ecf->dec/dot_general | solution.py:125
  251.1 8.7 %copy.48 = bf16[6144,512]{1,0:T(8,128)(2,1)} copy(bf16[6144,512]{0,1:T(8,128)(2,1)} %fusion.2) | data formatting | bytes 12582912
  260.6 8.3 %scatter_custom_fusion.2 = s32[4096]{0:T(1024)S(1)} fusion(s32[2048]{0:T(1024)S(1)} %reshape.373, s32[2048]{0:T(1024)S(1)} %reshape.381, s32[]{:T(128)} %constant.28.clone.1), kind=kCustom, calls=%fused_computation.72 | custom fusion | bytes 16388
  269.3 8.1 %scatter_custom_fusion.3 = s32[4096]{0:T(1024)S(1)} fusion(s32[2048]{0:T(1024)S(1)} %reshape.373, s32[2048]{0:T(1024)S(1)} %reshape.387, s32[]{:T(128)} %constant.28.clone.1), kind=kCustom, calls=%fused_computation.70 | custom fusion | bytes 16388
  277.4 4.7 %bitcast_convert_fusion = f32[32,1,512,192]{2,3,0,1:T(8,128)S(1)} fusion(bf16[32,1,512,192]{2,3,1,0:T(8,128)(2,1)} %all-to-all-done), kind=kLoop, calls=%fused_computation.12 | loop fusion | flops 3145728 | bytes 18874368 | tf_op jit(solution)/shard_map/convert_element_type | solution.py:116
  282.1 1.4 fusion.1
  284.5 76.2 %reduce-scatter.10.cloned.1.call-done = bf16[192,512]{1,0:T(8,128)(2,1)} async-done(((bf16[6144,512]{1,0:T(8,128)(2,1)}), bf16[192,512]{1,0:T(8,128)(2,1)}) %reduce-scatter.10.cloned.1.call-update) | async-done | bytes 196624
  360.7 1.8 copy.49
  362.5 4.9 %scatter_custom_fusion = f32[1024,192]{1,0:T(8,128)} fusion(s32[512]{0:T(512)S(1)} %bitcast.102, bf16[1,512,192]{2,1,0:T(8,128)(2,1)S(1)} %copy-done.4, f32[]{:T(128)} %constant.25.clone.1, bf16[192,512]{0,1:T(8,128)(2,1)} %copy.49, f32[512]{0:T(512)S(1)} %bitcast.101, f32[512]{0:T(512)S(1)} %add_divide_fusion), kind=kCustom, calls=%fused_computation.25 | custom fusion | flops 786432 | bytes 1249284 | tf_op jit(solution)/shard_map/scatter-add | solution.py:144
  367.4 2.1 convert_element_type.137
  369.5 37.1 %reduce-scatter.8.cloned.1.call-done = bf16[128,192]{1,0:T(8,128)(2,1)} async-done(((bf16[1024,192]{1,0:T(8,128)(2,1)}), bf16[128,192]{1,0:T(8,128)(2,1)}) %reduce-scatter.8.cloned.1.call-update) | async-done | bytes 49168 | tf_op jit(solution)/shard_map/reduce_scatter | solution.py:146
  406.6 1.6 copy.43
  (73 shorter events, 13.1 us)
Async XLA Ops:
  6.5 231.5 %copy-start = (bf16[1,256,6144]{2,1,0:T(8,128)(2,1)S(1)}, bf16[1,256,6144]{2,1,0:T(8,128)(2,1)}, u32[]{:S(2)}) copy-start(bf16[1,256,6144]{2,1,0:T(8,128)(2,1)} %param.28) | copy-start | bytes 9437188
  6.5 13.9 %copy-start.10 = (s32[2]{0:T(128)S(1)}, s32[2]{0:T(128)}, u32[]{:S(2)}) copy-start(s32[2]{0:T(128)} %constant.84) | copy-start | bytes 28
  6.5 14.0 %copy-start.11 = (s32[2]{0:T(128)S(1)}, s32[2]{0:T(128)}, u32[]{:S(2)}) copy-start(s32[2]{0:T(128)} %constant.87) | copy-start | bytes 28
  6.5 13.8 %copy-start.6 = (s32[1024,2]{0,1:T(2,128)S(1)}, s32[1024,2]{0,1:T(2,128)}, u32[]{:S(2)}) copy-start(s32[1024,2]{0,1:T(2,128)} %param.25) | copy-start | bytes 24580
  6.5 59.9 %copy-start.5 = (bf16[768,192]{0,1:T(8,128)(2,1)S(1)}, bf16[768,192]{0,1:T(8,128)(2,1)}, u32[]{:S(2)}) copy-start(bf16[768,192]{0,1:T(8,128)(2,1)} %param.21) | copy-start | bytes 884740
  6.5 59.9 %all-gather.2.cloned.1.call-start = ((), (), s32[]{:S(2)}) async-start(), calls=%async_computation.4 | async-start | bytes 1622016 | tf_op jit(solution)/shard_map/all_gather | solution.py:93
  15.4 119.5 %reduce-scatter.6.cloned.1.call-start = ((), (), s32[]{:S(2)}) async-start(), calls=%async_computation.5 | async-start | bytes 2359296 | tf_op jit(solution)/shard_map/reduce_scatter | solution.py:110
  139.3 7.8 %copy-start.8 = (f32[6144]{0:T(1024)S(1)}, f32[6144]{0:T(1024)}, u32[]{:S(2)}) copy-start(f32[6144]{0:T(1024)} %param.23) | copy-start | bytes 73732
  139.3 84.5 %all-to-all-start = ((bf16[32,1,512,192]{2,3,1,0:T(8,128)(2,1)}), bf16[32,1,512,192]{2,3,1,0:T(8,128)(2,1)}, u32[]{:S(2)}, u32[]{:S(2)}) async-start(bf16[32,1,512,192]{2,3,1,0:T(8,128)(2,1)} %stack.2), calls=%async_computation.1 | async-start | bytes 12582912 | tf_op jit(solution)/shard_map/all_to_all | solution.py:14
  146.9 213.8 %reduce-scatter.10.cloned.1.call-start = ((), (), s32[]{:S(2)}) async-start(), calls=%async_computation.7 | async-start | bytes 6488064
  228.3 7.1 %copy-start.3 = (bf16[1,6144,256]{2,1,0:T(8,128)(2,1)S(1)}, bf16[1,6144,256]{2,1,0:T(8,128)(2,1)}, u32[]{:S(2)}) copy-start(bf16[1,6144,256]{2,1,0:T(8,128)(2,1)} %param.26) | copy-start | bytes 9437188
  232.8 2.6 copy-start.2
  259.8 9.1 %copy-start.9 = (s32[2]{0:T(128)S(1)}, s32[2]{0:T(128)}, u32[]{:S(2)}) copy-start(s32[2]{0:T(128)} %constant.80.clone) | copy-start | bytes 28
  259.9 146.8 %reduce-scatter.8.cloned.1.call-start = ((), (), s32[]{:S(2)}) async-start(), calls=%async_computation.6 | async-start | bytes 589824 | tf_op jit(solution)/shard_map/reduce_scatter | solution.py:146
  282.1 1.5 copy-start.7
  282.1 126.1 %copy-start.1 = (bf16[1,256,6144]{2,1,0:T(8,128)(2,1)S(1)}, bf16[1,256,6144]{2,1,0:T(8,128)(2,1)}, u32[]{:S(2)}) copy-start(bf16[1,256,6144]{2,1,0:T(8,128)(2,1)} %param.28) | copy-start | bytes 9437188
  283.5 79.0 %copy-start.4 = (bf16[1,512,192]{2,1,0:T(8,128)(2,1)S(1)}, bf16[1,512,192]{2,1,0:T(8,128)(2,1)}, u32[]{:S(2)}) copy-start(bf16[1,512,192]{2,1,0:T(8,128)(2,1)} %reduce-scatter.6.cloned.1.call-done) | copy-start | bytes 589828
Sparse Core Ops, SparseCore 0:
  15.5 50.8 all-gather.1
  93.0 41.7 reduce-scatter.5
  260.0 100.6 reduce-scatter.9
  369.6 36.9 reduce-scatter.7
